TPU v7x, 512 devices: a whole 4x4x16 slice. The times are simulated.
512 devices in a mesh: row: 16 (over y, x), col: 32 (over z, core).
Axes of the slice: x: 4, y: 4, z: 16, core: 2. Of those that a mesh axis runs over, the one named last changes fastest.
Arguments:
- out_grad: bfloat16 [2048, 8192], P('col', 'row'), may hold values from -6 to 6
- hidden: bfloat16 [2048, 28672], P('row', 'col'), may hold values from -0.12988281 to 0.12988281
- weight: bfloat16 [28672, 8192], P('col', 'row'), may hold values from -0.03125 to 0.03125
Outputs:
- token_grad: bfloat16 [2048, 28672], P('row', 'col')
- weight_grad: bfloat16 [28672, 8192], P('col', 'row')
All inputs are finite; a program needn't handle non-finite values.
Results may differ from a plain program's by a relative error of at most 0.001.
Values may be sent and summed in bfloat16 or wider, within the bound.
A program may use at most 64 MiB of HBM per device.

v0:
```python
import jax
import jax.numpy as jnp
from jax import lax
from jax.sharding import PartitionSpec as P


def on_device(out_grad, hidden, weight):
    gathered = lax.all_gather(out_grad, "col", axis=0, tiled=True)
    cotangent = gathered
    weight_sum = lax.dot_general(
        lax.all_gather(hidden, "row", axis=0, tiled=True),
        cotangent,
        (((0,), (0,)), ((), ())),
        preferred_element_type=jnp.float32,
    )
    weight_grad = weight_sum.astype(jnp.bfloat16)
    own_full = lax.all_to_all(gathered, "row", split_axis=0, concat_axis=1, tiled=True)
    cotangent = own_full
    token_sum = lax.dot_general(
        cotangent,
        lax.all_gather(weight, "row", axis=1, tiled=True),
        (((1,), (1,)), ((), ())),
        preferred_element_type=jnp.float32,
    )
    return (token_sum.astype(jnp.bfloat16), weight_grad)


def solution(mesh):
    return jax.shard_map(
        on_device,
        mesh=mesh,
        in_specs=(P("col", "row"), P("row", "col"), P("col", "row")),
        out_specs=(P("row", "col"), P("col", "row")),
        check_vma=False,
    )
```

profile of v0, /device:TPU:1, one launch (start us, length us, event | category | flops | bytes accessed | tf_op | source)
XLA Modules:
  0.0 301.2 jit_solution(12447496459693819890)
XLA Ops:
  7.2 0.0 all-gather.4.cloned.1.call-start
  7.2 0.7 all-gather.4.cloned.1.call-update
  7.9 0.0 all-gather.8.cloned.1.call-start
  7.9 0.7 all-gather.8.cloned.1.call-update
  8.6 0.0 all-gather.6.cloned.1.call-start
  8.7 0.7 all-gather.6.cloned.1.call-update
  9.4 78.3 %all-gather.4.cloned.1.call-done = bf16[2048,512]{1,0:T(8,128)(2,1)} async-done(((bf16[64,512]{1,0:T(8,128)(2,1)}), bf16[2048,512]{1,0:T(8,128)(2,1)}) %all-gather.4.cloned.1.call-update) | async-done | bytes 2097168 | tf_op jit(solution)/shard_map/all_gather | solution.py:8
  87.7 37.9 %all_to_all.19 = bf16[16,128,512]{2,1,0:T(8,128)(2,1)S(1)} all-to-all(bf16[16,128,512]{2,1,0:T(8,128)(2,1)} %bitcast.9), channel_id=1, replica_groups=mesh['row'=16,'col'=32] {'row'}, dimensions={0} | all-to-all | bytes 4194304 | tf_op jit(solution)/shard_map/all_to_all | solution.py:17
  125.6 2.4 copy.5
  127.9 0.0 copy-start
  127.9 28.6 %all-gather.8.cloned.1.call-done = bf16[2048,896]{1,0:T(8,128)(2,1)} async-done(((bf16[128,896]{1,0:T(8,128)(2,1)}), bf16[2048,896]{1,0:T(8,128)(2,1)}) %all-gather.8.cloned.1.call-update) | async-done | bytes 3670032 | tf_op jit(solution)/shard_map/all_gather | solution.py:11
  156.6 5.7 %convolution_convert_fusion = bf16[896,512]{1,0:T(8,128)(2,1)} fusion(bf16[2048,896]{1,0:T(8,128)(2,1)} %all-gather.8.cloned.1.call-done, bf16[2048,512]{1,0:T(8,128)(2,1)} %all-gather.4.cloned.1.call-done), kind=kOutput, calls=%fused_computation | convolution fusion | flops 1879506944 | bytes 6684672 | tf_op jit(solution)/shard_map/dot_general | solution.py:10
  162.3 121.8 %all-gather.6.cloned.1.call-done = bf16[896,8192]{1,0:T(8,128)(2,1)} async-done(((bf16[896,512]{1,0:T(8,128)(2,1)}), bf16[896,8192]{1,0:T(8,128)(2,1)}) %all-gather.6.cloned.1.call-update) | async-done | bytes 14680080 | tf_op jit(solution)/shard_map/all_gather | solution.py:21
  284.1 0.0 copy-done
  284.1 10.6 %convolution_convert_fusion.1 = bf16[128,896]{1,0:T(8,128)(2,1)} fusion(bf16[128,8192]{0,1:T(8,128)(2,1)S(1)} %bitcast.8, bf16[896,8192]{1,0:T(8,128)(2,1)} %all-gather.6.cloned.1.call-done), kind=kOutput, calls=%fused_computation.1 | convolution fusion | flops 1879162880 | bytes 17006592 | tf_op jit(solution)/shard_map/dot_general | solution.py:19
Async XLA Ops:
  7.2 80.5 %all-gather.4.cloned.1.call-start = ((), (), s32[]{:S(2)}) async-start(), calls=%async_computation.1 | async-start | bytes 2162688 | tf_op jit(solution)/shard_map/all_gather | solution.py:8
  7.9 148.7 %all-gather.8.cloned.1.call-start = ((), (), s32[]{:S(2)}) async-start(), calls=%async_computation.3 | async-start | bytes 3899392 | tf_op jit(solution)/shard_map/all_gather | solution.py:11
  8.6 275.4 %all-gather.6.cloned.1.call-start = ((), (), s32[]{:S(2)}) async-start(), calls=%async_computation.2 | async-start | bytes 15597568 | tf_op jit(solution)/shard_map/all_gather | solution.py:21
  127.9 156.1 %copy-start = (bf16[128,16,512]{0,2,1:T(8,128)(2,1)S(1)}, bf16[128,16,512]{0,2,1:T(8,128)(2,1)}, u32[]{:S(2)}) copy-start(bf16[128,16,512]{0,2,1:T(8,128)(2,1)} %copy.5) | copy-start | bytes 6291460
Sparse Core Ops, SparseCore 0:
  10.1 77.5 all-gather.3
  90.7 65.8 all-gather.7
  159.6 124.4 all-gather.5
where the time goes:
time: 301 us
  waiting for transfers between devices  231 us (77%)
  blocking collectives  37.9 us (13%)
  matrix products  16.3 us (5%)
  between operations  13.7 us (5%)
    all_gather x1, waiting for transfers between devices, on_device(): lax.all_gather(weight, 'row', axis=1, tiled=True)  122 us
    all_gather x1, waiting for transfers between devices, on_device(): gathered = lax.all_gather(out_grad, 'col', axis=0, tiled=True)  78.3 us
    all_to_all x1, blocking collectives, on_device(): lax.all_to_all(gathered, 'row', split_axis=0, concat_axis=1, tiled=True)  37.9 us
    all_gather x1, waiting for transfers between devices, on_device(): lax.all_gather(hidden, 'row', axis=0, tiled=True)  28.6 us
    dot_general x1, matrix products, on_device(): lax.dot_general(cotangent, lax.all_gather(weight, 'row', axis=1, tiled=Tr...  10.6 us
  transfers between devices with their start and end apart: 3, of which 3 were waited for; matrix products, arithmetic and copies ran while one was open for 3% of the time, Pallas kernels for 0%

commit v1 on v0

--- a/solution.py
+++ b/solution.py
@@ -1,17 +1,30 @@
+import functools
 import jax
 import jax.numpy as jnp
 from jax import lax
 from jax.sharding import PartitionSpec as P
 
 
+def local_data_render(target, net_axis):
+    nd = lax.axis_size(net_axis)
+    odd = lax.all_to_all(
+        jnp.tile(target, tuple((nd if no == 0 else 1 for no in range(target.ndim)))),
+        net_axis,
+        split_axis=0,
+        concat_axis=0,
+        tiled=True,
+    )
+    return odd
+
+
+store_ways = functools.partial(local_data_render, net_axis="row")
+
+
 def on_device(out_grad, hidden, weight):
     gathered = lax.all_gather(out_grad, "col", axis=0, tiled=True)
     cotangent = gathered
     weight_sum = lax.dot_general(
-        lax.all_gather(hidden, "row", axis=0, tiled=True),
-        cotangent,
-        (((0,), (0,)), ((), ())),
-        preferred_element_type=jnp.float32,
+        store_ways(hidden), cotangent, (((0,), (0,)), ((), ())), preferred_element_type=jnp.float32
     )
     weight_grad = weight_sum.astype(jnp.bfloat16)
     own_full = lax.all_to_all(gathered, "row", split_axis=0, concat_axis=1, tiled=True)

time: 301 us -> 239 us (0.79)
  waiting for transfers between devices: 231 us -> 147 us
  blocking collectives: 37.9 us -> 50.3 us
  starting transfers between devices: 0.11 us -> 6.76 us
    all_gather x1, waiting for transfers between devices: 78.3 us -> 27.1 us  [on_device(): gathered = lax.all_gather(out_grad, 'col', axis=0, tiled=True)]
    all_gather x1, waiting for transfers between devices: 122 us -> 86.1 us  [on_device(): lax.all_gather(weight, 'row', axis=1, tiled=True)]
    all_to_all x0 -> x1, waiting for transfers between devices: none -> 32 us  [on_device(): lax.all_to_all(gathered, 'row', split_axis=0, concat_axis=1, tiled=True)]
    all_gather x1 -> x0, waiting for transfers between devices: 28.6 us -> none  [on_device(): lax.all_gather(hidden, 'row', axis=0, tiled=True)]
    all_to_all x1, blocking collectives: 37.9 us -> 50.3 us  [local_data_render(): lax.all_to_all(jnp.tile(target, tuple((nd if no == 0 else 1 for no in ran...]
    all_to_all x0 -> x1, starting transfers between devices: none -> 6.69 us  [on_device(): lax.all_to_all(gathered, 'row', split_axis=0, concat_axis=1, tiled=True)]
  transfers between devices with their start and end apart: 3 -> 3, of which waited for: 3 -> 3; matrix products, arithmetic and copies ran while one was open for 3% -> 4% of each run, Pallas kernels for 0% -> 0%
where the time goes in v1:
time: 239 us; the launch traced here: 238 us
  waiting for transfers between devices  147 us (62%)
  blocking collectives  50.3 us (21%)
  matrix products  16.9 us (7%)
  between operations  14.1 us (6%)
  starting transfers between devices  6.76 us (3%)
  local copies, waits for them, and re-layouts  3.81 us (2%)
    all_gather x1, waiting for transfers between devices, on_device(): lax.all_gather(weight, 'row', axis=1, tiled=True)  86.1 us
    all_to_all x1, blocking collectives, local_data_render(): lax.all_to_all(jnp.tile(target, tuple((nd if no == 0 else 1 for no in ran...  50.3 us
    all_to_all x1, waiting for transfers between devices, on_device(): lax.all_to_all(gathered, 'row', split_axis=0, concat_axis=1, tiled=True)  32 us
    all_gather x1, waiting for transfers between devices, on_device(): gathered = lax.all_gather(out_grad, 'col', axis=0, tiled=True)  27.1 us
    dot_general x1, matrix products, on_device(): lax.dot_general(cotangent, lax.all_gather(weight, 'row', axis=1, tiled=Tr...  11.2 us
    all_to_all x1, starting transfers between devices, on_device(): lax.all_to_all(gathered, 'row', split_axis=0, concat_axis=1, tiled=True)  6.69 us
    dot_general x1, matrix products, on_device(): lax.dot_general(store_ways(hidden), cotangent, (((0,), (0,)), ((), ())),...  5.72 us
  transfers between devices with their start and end apart: 3, of which 3 were waited for; matrix products, arithmetic and copies ran while one was open for 4% of the time, Pallas kernels for 0%

profile of v1, /device:TPU:1, one launch (start us, length us, event | category | flops | bytes accessed | tf_op | source)
XLA Modules:
  0.0 238.4 jit_solution(16517772892827461739)
XLA Ops:
  7.2 0.0 all-gather.3.cloned.1.call-start
  7.2 0.7 all-gather.3.cloned.1.call-update
  7.9 0.0 all-gather.5.cloned.1.call-start
  7.9 0.7 all-gather.5.cloned.1.call-update
  8.6 1.4 tile.2
  10.1 50.3 %all_to_all.28 = bf16[16,128,896]{2,1,0:T(8,128)(2,1)} all-to-all(bf16[16,128,896]{2,1,0:T(8,128)(2,1)S(1)} %tile.2), channel_id=1, replica_groups=mesh['row'=16,'col'=32] {'row'}, dimensions={0} | all-to-all | bytes 7340032 | tf_op jit(solution)/shard_map/all_to_all | solution.py:10
  60.4 27.1 %all-gather.3.cloned.1.call-done = bf16[2048,512]{1,0:T(8,128)(2,1)} async-done(((bf16[64,512]{1,0:T(8,128)(2,1)}), bf16[2048,512]{1,0:T(8,128)(2,1)}) %all-gather.3.cloned.1.call-update) | async-done | bytes 2097168 | tf_op jit(solution)/shard_map/all_gather | solution.py:24
  87.4 6.7 %all-to-all-start = ((bf16[16,128,512]{2,1,0:T(8,128)(2,1)}), bf16[16,128,512]{2,1,0:T(8,128)(2,1)S(1)}, u32[]{:S(2)}, u32[]{:S(2)}) async-start(bf16[16,128,512]{2,1,0:T(8,128)(2,1)} %bitcast.11), calls=%async_computation | async-start | bytes 4194304 | tf_op jit(solution)/shard_map/all_to_all | solution.py:30
  94.1 5.7 %convolution_convert_fusion = bf16[896,512]{1,0:T(8,128)(2,1)} fusion(bf16[2048,896]{1,0:T(8,128)(2,1)} %bitcast.10, bf16[2048,512]{1,0:T(8,128)(2,1)} %all-gather.3.cloned.1.call-done), kind=kOutput, calls=%fused_computation | convolution fusion | flops 1879506944 | bytes 6684672 | tf_op jit(solution)/shard_map/dot_general | solution.py:26
  99.9 32.0 %all-to-all-done = bf16[16,128,512]{2,1,0:T(8,128)(2,1)S(1)} async-done(((bf16[16,128,512]{2,1,0:T(8,128)(2,1)}), bf16[16,128,512]{2,1,0:T(8,128)(2,1)S(1)}, u32[]{:S(2)}, u32[]{:S(2)}) %all-to-all-start) | async-done | bytes 2097184 | tf_op jit(solution)/shard_map/all_to_all | solution.py:30
  131.9 2.4 copy.5
  134.2 86.1 %all-gather.5.cloned.1.call-done = bf16[896,8192]{1,0:T(8,128)(2,1)} async-done(((bf16[896,512]{1,0:T(8,128)(2,1)}), bf16[896,8192]{1,0:T(8,128)(2,1)}) %all-gather.5.cloned.1.call-update) | async-done | bytes 14680080 | tf_op jit(solution)/shard_map/all_gather | solution.py:34
  220.3 11.2 %convolution_convert_fusion.1 = bf16[128,896]{1,0:T(8,128)(2,1)} fusion(bf16[128,8192]{0,1:T(8,128)(2,1)} %bitcast.9, bf16[896,8192]{1,0:T(8,128)(2,1)} %all-gather.5.cloned.1.call-done), kind=kOutput, calls=%fused_computation.1 | convolution fusion | flops 1879162880 | bytes 17006592 | tf_op jit(solution)/shard_map/dot_general | solution.py:32
Async XLA Ops:
  7.2 80.3 %all-gather.3.cloned.1.call-start = ((), (), s32[]{:S(2)}) async-start(), calls=%async_computation.2 | async-start | bytes 2162688 | tf_op jit(solution)/shard_map/all_gather | solution.py:24
  7.9 212.4 %all-gather.5.cloned.1.call-start = ((), (), s32[]{:S(2)}) async-start(), calls=%async_computation.3 | async-start | bytes 15597568 | tf_op jit(solution)/shard_map/all_gather | solution.py:34
  87.4 44.4 %all-to-all-start = ((bf16[16,128,512]{2,1,0:T(8,128)(2,1)}), bf16[16,128,512]{2,1,0:T(8,128)(2,1)S(1)}, u32[]{:S(2)}, u32[]{:S(2)}) async-start(bf16[16,128,512]{2,1,0:T(8,128)(2,1)} %bitcast.11), calls=%async_computation | async-start | bytes 4194304 | tf_op jit(solution)/shard_map/all_to_all | solution.py:30
Sparse Core Ops, SparseCore 0:
  10.1 77.2 all-gather.2
  90.4 129.8 all-gather.4
